TPU v7x, 32 devices: a whole 2x2x4 slice. The times are simulated.
32 devices in a mesh: row: 8 (over z, x), col: 4 (over y, core).
Axes of the slice: x: 2, y: 2, z: 4, core: 2. Of those that a mesh axis runs over, the one named last changes fastest.
Arguments:
- charges: float32 [32768], P(('row', 'col')), may hold values from -0.5 to 1.5
- structure_id: int32 [32768], P(('row', 'col')), may hold values from 0 to 255, as said below
- live_count: int32 [32], P(('row', 'col')), may hold values from 512 to 1024, as said below
- cell_index: int32 [3, 32768], P(None, ('row', 'col')), may hold values from 0 to 255, as said below
- fraction: float32 [3, 32768], P(None, ('row', 'col')), may hold values from 0 to 1
- influence: float32 [256, 64, 64], P('col', 'row'), may hold values from 0.1 to 10
Outputs:
- forces: float32 [3, 32768], P(None, ('row', 'col'))
- atom_energy: float32 [32768], P(('row', 'col'))
Inputs may be any that keep to these rules, and one draw needn't show every extreme that they name: `structure_id`: devices are numbered row-major over (row, col). Slots 0 to 7 of device d are live and belong to fragments d * 8 to d * 8 + 7, so every fragment has a live atom; every other slot names a fragment of its own device, of one of the four devices beside it along row or col (wrapping around), or of the device whose number is d plus half the number of devices (wrapping around). Device d's live atoms are its first live_count[d] slots; the count reaches 1024 on some device in every draw. `cell_index`: the atom slots of the device at (row r, col c) lie in its mesh block: first index from r * 8 to r * 8 + 7, second from c * 16 to c * 16 + 15; the third is anywhere.
All inputs are finite; a program needn't handle non-finite values.
Results may differ from a plain program's by a relative error of at most 0.000065.
Values sent between devices are 32-bit elements; how exact they have to be, the bound alone decides.
A program may use at most 64 MiB of HBM per device.

v0:
```python
import math
import jax
import jax.numpy as jnp
from jax import lax
from jax.sharding import PartitionSpec as P

CX = 8
CY = 16
NZ = 256
S_DEV = 8
highest = lax.Precision.HIGHEST


def passed_along(block, axis, distance):
    devices = range(lax.axis_size(axis))
    route = [((i - distance) % len(devices), i) for i in devices]
    return lax.ppermute(block, axis, route)


def spline_weights(fraction):
    remain = 1.0 - fraction
    square = fraction * fraction
    cubic_term = square * fraction
    values = [
        remain * remain * remain / 6.0,
        (3.0 * cubic_term - 6.0 * square + 4.0) / 6.0,
        (-3.0 * cubic_term + 3.0 * square + 3.0 * fraction + 1.0) / 6.0,
        cubic_term / 6.0,
    ]
    slopes = [
        -0.5 * remain * remain,
        0.5 * (3.0 * square - 4.0 * fraction),
        0.5 * (-3.0 * square + 2.0 * fraction + 1.0),
        0.5 * square,
    ]
    return (values, slopes)


def place_weights(weights, local, width, period):
    columns = lax.broadcasted_iota(jnp.int32, (local.shape[0], width), 1)
    result = jnp.zeros((local.shape[0], width), jnp.float32)
    for offset in range(4):
        target = (local + offset) % period
        result = result + jnp.where(columns == target[:, None], weights[offset][:, None], 0.0)
    return result


def dft_tables(length):
    counter = lax.iota(jnp.int32, length)
    product = counter[:, None] * counter[None, :] % length
    angle = 2.0 * math.pi / length * product.astype(jnp.float32)
    return (jnp.cos(angle), jnp.sin(angle))


def rotate_pair(real_part, imag_part, pattern, cosine, sine, direction):
    real_cos = jnp.einsum(pattern, real_part, cosine, precision=highest)
    real_sin = jnp.einsum(pattern, real_part, sine, precision=highest)
    imag_cos = jnp.einsum(pattern, imag_part, cosine, precision=highest)
    imag_sin = jnp.einsum(pattern, imag_part, sine, precision=highest)
    return (real_cos - direction * imag_sin, imag_cos + direction * real_sin)


def body(charges, structure_id, live_count, cell_index, fraction, influence):
    atom_total = charges.shape[0]
    row_count = lax.axis_size("row")
    col_count = lax.axis_size("col")
    mesh_x = CX * row_count
    mesh_y = CY * col_count
    structures = S_DEV * row_count * col_count
    local_x = cell_index[0] - lax.axis_index("row") * CX
    local_y = cell_index[1] - lax.axis_index("col") * CY
    live = (lax.iota(jnp.int32, atom_total) < live_count[0]).astype(jnp.float32)
    wx_val, wx_slope = spline_weights(fraction[0])
    wy_val, wy_slope = spline_weights(fraction[1])
    wz_val, wz_slope = spline_weights(fraction[2])
    big_period = 4 * (CX + CY + 8)
    x_rows = place_weights(wx_val, local_x, CX + 3, big_period)
    x_slope_rows = place_weights(wx_slope, local_x, CX + 3, big_period)
    y_rows = place_weights(wy_val, local_y, CY + 3, big_period)
    y_slope_rows = place_weights(wy_slope, local_y, CY + 3, big_period)
    z_rows = place_weights(wz_val, cell_index[2], NZ, NZ)
    z_slope_rows = place_weights(wz_slope, cell_index[2], NZ, NZ)
    plane = (y_rows[:, :, None] * x_rows[:, None, :]).reshape(atom_total, -1)
    charge_sums = jax.ops.segment_sum(charges * live, structure_id, num_segments=structures)
    live_sums = jax.ops.segment_sum(live, structure_id, num_segments=structures)
    totals, counts = lax.psum((charge_sums, live_sums), ("row", "col"))
    neutral = (charges - jnp.take(totals / counts, structure_id)) * live
    spread_grid = lax.dot_general(
        plane,
        neutral[:, None] * z_rows,
        (((0,), (0,)), ((), ())),
        precision=highest,
        preferred_element_type=jnp.float32,
    )
    extended = spread_grid.reshape(CY + 3, CX + 3, NZ)
    spill_x = passed_along(extended[:, CX:, :], "row", 1)
    extended = extended[:, :CX, :].at[:, :3, :].add(spill_x)
    spill_y = passed_along(extended[CY:], "col", 1)
    density = extended[:CY].at[:3].add(spill_y)
    cos_z, sin_z = dft_tables(NZ)
    cos_y, sin_y = dft_tables(mesh_y)
    cos_x, sin_x = dft_tables(mesh_x)
    real_z = jnp.einsum("yxz,zk->kxy", density, cos_z, precision=highest)
    imag_z = -jnp.einsum("yxz,zk->kxy", density, sin_z, precision=highest)
    columns = lax.all_to_all(
        jnp.stack([real_z, imag_z]), "col", split_axis=1, concat_axis=3, tiled=True
    )
    real_y, imag_y = rotate_pair(columns[0], columns[1], "zxy,yk->zkx", cos_y, sin_y, -1.0)
    rows = lax.all_to_all(
        jnp.stack([real_y, imag_y]), "row", split_axis=2, concat_axis=3, tiled=True
    )
    real_x, imag_x = rotate_pair(rows[0], rows[1], "zyx,xk->zyk", cos_x, sin_x, -1.0)
    scale = influence / float(mesh_x * mesh_y * NZ)
    real_x = real_x * scale
    imag_x = imag_x * scale
    back_x, back_x_imag = rotate_pair(real_x, imag_x, "zyk,kx->zyx", cos_x, sin_x, 1.0)
    returned = lax.all_to_all(
        jnp.stack([back_x, back_x_imag]), "row", split_axis=3, concat_axis=2, tiled=True
    )
    back_y, back_y_imag = rotate_pair(returned[0], returned[1], "zkx,ky->zxy", cos_y, sin_y, 1.0)
    whole_z = lax.all_to_all(
        jnp.stack([back_y, back_y_imag]), "col", split_axis=3, concat_axis=1, tiled=True
    )
    potential = jnp.einsum("kxy,kz->yxz", whole_z[0], cos_z, precision=highest) - jnp.einsum(
        "kxy,kz->yxz", whole_z[1], sin_z, precision=highest
    )
    upper_x = passed_along(potential[:, :3, :], "row", -1)
    widened = jnp.concatenate([potential, upper_x], axis=1)
    upper_y = passed_along(widened[:3], "col", -1)
    widened = jnp.concatenate([widened, upper_y], axis=0).reshape(-1, NZ)
    sampled = lax.dot_general(
        jnp.concatenate([z_rows, z_slope_rows], axis=0),
        widened,
        (((1,), (1,)), ((), ())),
        precision=highest,
        preferred_element_type=jnp.float32,
    )
    sample_val = sampled[:atom_total]
    sample_slope = sampled[atom_total:]
    plane_dx = (y_rows[:, :, None] * x_slope_rows[:, None, :]).reshape(atom_total, -1)
    plane_dy = (y_slope_rows[:, :, None] * x_rows[:, None, :]).reshape(atom_total, -1)
    value = jnp.sum(plane * sample_val, axis=1)
    grad_x = jnp.sum(plane_dx * sample_val, axis=1)
    grad_y = jnp.sum(plane_dy * sample_val, axis=1)
    grad_z = jnp.sum(plane * sample_slope, axis=1)
    atom_energy = 0.5 * neutral * value
    forces = -neutral[None, :] * jnp.stack([grad_x, grad_y, grad_z])
    return (forces, atom_energy)


def solution(mesh):
    placed = (
        P(("row", "col")),
        P(("row", "col")),
        P(("row", "col")),
        P(None, ("row", "col")),
        P(None, ("row", "col")),
        P("col", "row", None),
    )
    return jax.shard_map(
        body,
        mesh=mesh,
        in_specs=placed,
        out_specs=(P(None, ("row", "col")), P(("row", "col"))),
        check_vma=False,
    )
```

profile of v0, /device:TPU:3, one launch (start us, length us, event | category | flops | bytes accessed | tf_op | source)
XLA Modules:
  0.0 171.7 jit_solution(16986416854421868476)
XLA Ops:
  1.3 0.7 fusion.132
  2.0 0.7 fusion.131
  2.7 7.7 %scatter_custom_fusion = f32[256]{0:T(256)S(1)} fusion(s32[1024]{0:T(1024)} %param.11, f32[1024]{0:T(1024)S(1)} %fusion.131, f32[]{:T(128)} %constant.237.clone.1), kind=kCustom, calls=%fused_computation.243 | custom fusion | flops 1024 | bytes 1536 | tf_op jit(solution)/shard_map/scatter-add | solution.py:84
  10.4 7.7 %scatter_custom_fusion.1 = f32[256]{0:T(256)S(1)} fusion(s32[1024]{0:T(1024)} %param.11, f32[1024]{0:T(1024)S(1)} %fusion.130, f32[]{:T(128)} %constant.237.clone.1), kind=kCustom, calls=%fused_computation.241 | custom fusion | flops 1024 | bytes 1536 | tf_op jit(solution)/shard_map/scatter-add | solution.py:85
  18.2 0.8 fusion.226
  19.1 0.8 fusion.227
  20.1 1.9 %broadcast_multiply_fusion.2 = (f32[1024,19,11]{0,2,1:T(8,128)}, f32[1024,19,11]{0,2,1:T(8,128)S(1)}, f32[1024,19,11]{0,2,1:T(8,128)}) fusion(f32[1024,11]{0,1:T(8,128)S(1)} %get-tuple-element.45, f32[1024,19]{0,1:T(8,128)S(1)} %get-tuple-element.48, f32[1024,11]{0,1:T(8,128)S(1)} %get-tuple-element.46, f32[1024,19]{0,1:T(8,128)S(1)} %get-tuple-element.47), kind=kLoop, calls=%fused_computation.46 | loop fusion | flops 642048 | bytes 2813952 | tf_op jit(solution)/shard_map/mul | solution.py:140
  22.3 39.6 %all-reduce = (f32[256]{0:T(256)S(1)}, f32[256]{0:T(256)S(1)}) all-reduce(f32[256]{0:T(256)S(1)} %scatter_custom_fusion, f32[256]{0:T(256)S(1)} %scatter_custom_fusion.1), channel_id=1, replica_groups=mesh['row'=8,'col'=4] {'row','col'}, use_global_device_ids=true, to_apply=%region_1.2 | all-reduce | flops 512 | bytes 4096 | tf_op jit(solution)/shard_map/psum | solution.py:86
  61.9 6.8 %gather_fusion = f32[1024]{0:T(1024)S(1)} fusion(f32[256]{0:T(256)S(1)} %div.45, s32[1024]{0:T(1024)S(1)} %fusion.132), kind=kCustom, calls=%fused_computation | custom fusion | bytes 12288 | tf_op jit(solution)/shard_map/jit(_take)/gather | solution.py:87
  68.8 0.6 multiply_multiply_fusion.2
  69.5 2.2 %fusion.17 = f32[19,11,256]{2,1,0:T(8,128)S(1)} fusion(f32[19,11,1024]{2,1,0:T(8,128)S(1)} %dot_general.71, f32[1024]{0:T(1024)S(1)} %get-tuple-element.94, f32[1024]{0:T(1024)S(1)} %get-tuple-element.79, s32[1024]{0:T(1024)S(1)} %get-tuple-element.84, f32[1024]{0:T(1024)S(1)} %get-tuple-element.78, s32[1024]{0:T(1024)S(1)} %get-tuple-element.83, ...), kind=kOutput, calls=%fused_computation.30 | convolution fusion | flops 660602880 | bytes 1106944 | tf_op jit(solution)/shard_map/dot_general | solution.py:88
  71.7 1.4 collective-permute-start
  73.1 1.9 %collective-permute-done = f32[19,3,256]{2,1,0:T(4,128)S(1)} collective-permute-done((f32[19,3,256]{2,1,0:T(4,128)S(1)}, f32[19,3,256]{2,1,0:T(4,128)S(1)}, u32[]{:S(2)}, u32[]{:S(2)}) %collective-permute-start) | collective-permute-done | bytes 58400 | tf_op jit(solution)/shard_map/ppermute | solution.py:17
  75.3 3.8 %collective-permute-start.1 = (f32[3,8,256]{2,1,0:T(8,128)S(1)}, f32[3,8,256]{2,1,0:T(8,128)S(1)}, u32[]{:S(2)}, u32[]{:S(2)}) collective-permute-start(f32[3,8,256]{2,1,0:T(8,128)S(1)} %slice.156), channel_id=1, source_target_pairs={{3,0},{0,1},{1,2},{2,3},{7,4},{4,5},{5,6},{6,7},{11,8},{8,9},{9,10... | collective-permute-start | bytes 73736 | tf_op jit(solution)/shard_map/ppermute | solution.py:17
  79.1 0.9 collective-permute-done.1
  80.1 1.3 fusion.16
  81.4 1.3 convolution_bitcast_fusion
  82.7 1.3 copy.81
  84.0 0.7 reshape.1016
  84.8 9.5 %all_to_all.60 = f32[4,1,16384]{2,1,0:T(1,128)S(1)} all-to-all(f32[4,1,16384]{2,1,0:T(1,128)S(1)} %reshape.1016), channel_id=1, replica_groups=mesh['row'=8,'col'=4] {'col'}, dimensions={0} | all-to-all | bytes 524288 | tf_op jit(solution)/shard_map/all_to_all | solution.py:105
  94.2 0.6 broadcast.1325
  94.8 1.3 reduce.4
  96.1 0.7 reshape.1017
  96.8 1.1 copy.128
  98.0 0.5 fusion.73
  98.6 0.5 fusion.71
  99.1 0.6 fusion.15
  99.7 0.5 fusion.13
  100.6 0.3 reshape.1018
  100.9 12.2 %all_to_all.61 = f32[8,1,8192]{2,1,0:T(1,128)S(1)} all-to-all(f32[8,1,8192]{2,1,0:T(1,128)S(1)} %reshape.1018), channel_id=1, replica_groups=mesh['row'=8,'col'=4] {'row'}, dimensions={0} | all-to-all | bytes 524288 | tf_op jit(solution)/shard_map/all_to_all | solution.py:109
  113.2 1.2 reduce.5
  114.7 0.6 fusion.29
  115.4 0.6 fusion.25
  116.0 0.6 fusion.11
  116.7 0.6 fusion.9
  117.3 0.5 fusion.65
  117.8 0.5 fusion.68
  118.3 0.5 fusion.6
  118.8 0.5 fusion.7
  119.6 0.3 reshape.1020
  120.0 11.0 %all_to_all.62 = f32[8,1,8192]{2,1,0:T(1,128)S(1)} all-to-all(f32[8,1,8192]{2,1,0:T(1,128)S(1)} %reshape.1020), channel_id=1, replica_groups=mesh['row'=8,'col'=4] {'row'}, dimensions={0} | all-to-all | bytes 524288 | tf_op jit(solution)/shard_map/all_to_all | solution.py:117
  131.0 1.2 reduce.6
  132.9 0.5 fusion.63
  133.5 0.5 fusion.61
  134.1 0.5 fusion.5
  134.6 0.5 fusion.4
  135.7 11.2 %all_to_all.63 = f32[4,1,16384]{2,1,0:T(1,128)S(1)} all-to-all(f32[4,1,16384]{2,1,0:T(1,128)S(1)} %reshape.1022), channel_id=1, replica_groups=mesh['row'=8,'col'=4] {'col'}, dimensions={0} | all-to-all | bytes 524288 | tf_op jit(solution)/shard_map/all_to_all | solution.py:121
  146.9 1.3 reduce.7
  149.1 1.3 fusion.45
  150.8 1.3 fusion.42
  152.1 0.3 collective-permute-start.2
  152.5 3.6 %collective-permute-done.2 = f32[16,3,256]{2,0,1:T(8,128)S(1)} collective-permute-done((f32[16,3,256]{2,0,1:T(8,128)S(1)}, f32[16,3,256]{2,0,1:T(8,128)S(1)}, u32[]{:S(2)}, u32[]{:S(2)}) %collective-permute-start.2) | collective-permute-done | bytes 49184 | tf_op jit(solution)/shard_map/ppermute | solution.py:17
  156.0 0.6 pad_maximum_fusion.5
  156.7 2.2 %collective-permute-start.3 = (f32[3,11,256]{2,0,1:T(4,128)}, f32[3,11,256]{2,0,1:T(4,128)}, u32[]{:S(2)}, u32[]{:S(2)}) collective-permute-start(f32[3,11,256]{2,0,1:T(4,128)} %pad_maximum_fusion.5), channel_id=1, source_target_pairs={{1,0},{2,1},{3,2},{0,3},{5,4},{6,5},{7,6},{4,7},{9,8},{10,9},{11,1... | collective-permute-start | bytes 101384 | tf_op jit(solution)/shard_map/ppermute | solution.py:17
  158.9 3.1 %select_add_fusion.1 = (f32[1024,256]{1,0:T(8,128)}, f32[1024,256]{1,0:T(8,128)}) fusion(f32[1024]{0:T(1024)S(1)} %copy-done.16, s32[1024]{0:T(1024)S(1)} %copy-done.26, f32[1024]{0:T(1024)S(1)} %copy-done.14, s32[1024]{0:T(1024)S(1)} %copy-done.24, f32[1024]{0:T(1024)S(1)} %copy-done.18, s32[1024]{0:T(1024)S(1)} %copy-done.22, f32[1024]{0:T(1024)S(1)} %copy-done.11, ...), kind=kLoop, calls=%fused_computation.34 | loop fusion | flops 4718592 | bytes 2146304 | tf_op jit(solution)/shard_map/add | solution.py:44
  162.0 1.0 mul.759
  163.1 0.6 copy-done
  163.7 1.0 mul.815
  164.7 0.9 pad_maximum_fusion.3
  165.7 0.7 reshape.969
  166.4 3.3 %fusion = f32[2048,209]{0,1:T(8,128)S(1)} fusion(f32[209,256]{1,0:T(8,128)} %reshape.969, f32[1024,256]{1,0:T(8,128)S(1)} %copy-done.3, f32[1024,256]{1,0:T(8,128)S(1)} %copy-done.2), kind=kOutput, calls=%fused_computation.3 | convolution fusion | flops 1315438592 | bytes 4023296 | tf_op jit(solution)/shard_map/dot_general | solution.py:131
  169.8 0.5 multiply_reduce_fusion
  170.4 0.6 multiply_multiply_fusion.21
  171.0 0.6 maximum_multiply_fusion
  (113 shorter events, 4.7 us)
Async XLA Ops:
  19.1 50.4 %copy-start.19 = (s32[1024]{0:T(1024)}, s32[1024]{0:T(1024)S(1)}, u32[]{:S(2)}) copy-start(s32[1024]{0:T(1024)S(1)} %get-tuple-element.81) | copy-start | bytes 12292
  19.1 50.4 %copy-start.21 = (s32[1024]{0:T(1024)}, s32[1024]{0:T(1024)S(1)}, u32[]{:S(2)}) copy-start(s32[1024]{0:T(1024)S(1)} %get-tuple-element.82) | copy-start | bytes 12292
  19.1 50.4 %copy-start.23 = (s32[1024]{0:T(1024)}, s32[1024]{0:T(1024)S(1)}, u32[]{:S(2)}) copy-start(s32[1024]{0:T(1024)S(1)} %get-tuple-element.83) | copy-start | bytes 12292
  19.1 50.4 %copy-start.25 = (s32[1024]{0:T(1024)}, s32[1024]{0:T(1024)S(1)}, u32[]{:S(2)}) copy-start(s32[1024]{0:T(1024)S(1)} %get-tuple-element.84) | copy-start | bytes 12292
  61.9 6.8 %copy-start.29 = (f32[1024]{0:T(1024)S(1)}, f32[1024]{0:T(1024)}, u32[]{:S(2)}) copy-start(f32[1024]{0:T(1024)} %param.10) | copy-start | bytes 12292
  61.9 6.9 %copy-start.30 = (s32[1024]{0:T(1024)S(1)}, s32[1024]{0:T(1024)}, u32[]{:S(2)}) copy-start(s32[1024]{0:T(1024)} %param.11) | copy-start | bytes 12292
  69.4 2.3 %copy-start.10 = (f32[1024]{0:T(1024)}, f32[1024]{0:T(1024)S(1)}, u32[]{:S(2)}) copy-start(f32[1024]{0:T(1024)S(1)} %get-tuple-element.76) | copy-start | bytes 12292
  69.4 2.3 %copy-start.13 = (f32[1024]{0:T(1024)}, f32[1024]{0:T(1024)S(1)}, u32[]{:S(2)}) copy-start(f32[1024]{0:T(1024)S(1)} %get-tuple-element.78) | copy-start | bytes 12292
  69.4 2.3 %copy-start.15 = (f32[1024]{0:T(1024)}, f32[1024]{0:T(1024)S(1)}, u32[]{:S(2)}) copy-start(f32[1024]{0:T(1024)S(1)} %get-tuple-element.79) | copy-start | bytes 12292
  69.4 2.3 %copy-start.17 = (f32[1024]{0:T(1024)}, f32[1024]{0:T(1024)S(1)}, u32[]{:S(2)}) copy-start(f32[1024]{0:T(1024)S(1)} %get-tuple-element.80) | copy-start | bytes 12292
  69.4 2.3 %copy-start.27 = (f32[1024]{0:T(1024)}, f32[1024]{0:T(1024)S(1)}, u32[]{:S(2)}) copy-start(f32[1024]{0:T(1024)S(1)} %get-tuple-element.94) | copy-start | bytes 12292
  71.7 3.3 %collective-permute-start = (f32[19,3,256]{2,1,0:T(4,128)S(1)}, f32[19,3,256]{2,1,0:T(4,128)S(1)}, u32[]{:S(2)}, u32[]{:S(2)}) collective-permute-start(f32[19,3,256]{2,1,0:T(4,128)S(1)} %slice.153), channel_id=1, source_target_pairs={{28,0},{0,4},{4,8},{8,12},{12,16},{16,20},{20,24},{24,28},{29,1},{... | collective-permute-start | bytes 175112 | tf_op jit(solution)/shard_map/ppermute | solution.py:17
  75.3 4.8 %collective-permute-start.1 = (f32[3,8,256]{2,1,0:T(8,128)S(1)}, f32[3,8,256]{2,1,0:T(8,128)S(1)}, u32[]{:S(2)}, u32[]{:S(2)}) collective-permute-start(f32[3,8,256]{2,1,0:T(8,128)S(1)} %slice.156), channel_id=1, source_target_pairs={{3,0},{0,1},{1,2},{2,3},{7,4},{4,5},{5,6},{6,7},{11,8},{8,9},{9,10... | collective-permute-start | bytes 73736 | tf_op jit(solution)/shard_map/ppermute | solution.py:17
  114.7 1.3 copy-start.6
  150.4 8.5 %copy-start.7 = (f32[1024]{0:T(1024)S(1)}, f32[1024]{0:T(1024)}, u32[]{:S(2)}) copy-start(f32[1024]{0:T(1024)} %get-tuple-element.73) | copy-start | bytes 12292
  150.4 8.5 %copy-start.8 = (f32[1024]{0:T(1024)S(1)}, f32[1024]{0:T(1024)}, u32[]{:S(2)}) copy-start(f32[1024]{0:T(1024)} %get-tuple-element.74) | copy-start | bytes 12292
  150.4 8.5 %copy-start.9 = (f32[1024]{0:T(1024)S(1)}, f32[1024]{0:T(1024)}, u32[]{:S(2)}) copy-start(f32[1024]{0:T(1024)} %get-tuple-element.75) | copy-start | bytes 12292
  150.4 8.5 %copy-start.11 = (f32[1024]{0:T(1024)S(1)}, f32[1024]{0:T(1024)}, u32[]{:S(2)}) copy-start(f32[1024]{0:T(1024)} %copy-done.10) | copy-start | bytes 12292
  150.4 8.5 %copy-start.12 = (f32[1024]{0:T(1024)S(1)}, f32[1024]{0:T(1024)}, u32[]{:S(2)}) copy-start(f32[1024]{0:T(1024)} %get-tuple-element.77) | copy-start | bytes 12292
  150.4 8.5 %copy-start.14 = (f32[1024]{0:T(1024)S(1)}, f32[1024]{0:T(1024)}, u32[]{:S(2)}) copy-start(f32[1024]{0:T(1024)} %copy-done.13) | copy-start | bytes 12292
  150.4 8.5 %copy-start.16 = (f32[1024]{0:T(1024)S(1)}, f32[1024]{0:T(1024)}, u32[]{:S(2)}) copy-start(f32[1024]{0:T(1024)} %copy-done.15) | copy-start | bytes 12292
  150.4 8.5 %copy-start.18 = (f32[1024]{0:T(1024)S(1)}, f32[1024]{0:T(1024)}, u32[]{:S(2)}) copy-start(f32[1024]{0:T(1024)} %copy-done.17) | copy-start | bytes 12292
  150.4 8.5 %copy-start.20 = (s32[1024]{0:T(1024)S(1)}, s32[1024]{0:T(1024)}, u32[]{:S(2)}) copy-start(s32[1024]{0:T(1024)} %copy-done.19) | copy-start | bytes 12292
  150.5 8.5 %copy-start.22 = (s32[1024]{0:T(1024)S(1)}, s32[1024]{0:T(1024)}, u32[]{:S(2)}) copy-start(s32[1024]{0:T(1024)} %copy-done.21) | copy-start | bytes 12292
  150.5 8.5 %copy-start.24 = (s32[1024]{0:T(1024)S(1)}, s32[1024]{0:T(1024)}, u32[]{:S(2)}) copy-start(s32[1024]{0:T(1024)} %copy-done.23) | copy-start | bytes 12292
  150.5 8.5 %copy-start.26 = (s32[1024]{0:T(1024)S(1)}, s32[1024]{0:T(1024)}, u32[]{:S(2)}) copy-start(s32[1024]{0:T(1024)} %copy-done.25) | copy-start | bytes 12292
  152.1 9.9 %copy-start.1 = (f32[1024,19,11]{0,2,1:T(8,128)S(1)}, f32[1024,19,11]{0,2,1:T(8,128)}, u32[]{:S(2)}) copy-start(f32[1024,19,11]{0,2,1:T(8,128)} %get-tuple-element.42) | copy-start | bytes 2568196
  152.1 3.9 %collective-permute-start.2 = (f32[16,3,256]{2,0,1:T(8,128)S(1)}, f32[16,3,256]{2,0,1:T(8,128)S(1)}, u32[]{:S(2)}, u32[]{:S(2)}) collective-permute-start(f32[16,3,256]{2,0,1:T(8,128)S(1)} %slice.165), channel_id=1, source_target_pairs={{4,0},{8,4},{12,8},{16,12},{20,16},{24,20},{28,24},{0,28},{5,1},{9... | collective-permute-start | bytes 147464 | tf_op jit(solution)/shard_map/ppermute | solution.py:17
  156.7 8.0 %collective-permute-start.3 = (f32[3,11,256]{2,0,1:T(4,128)}, f32[3,11,256]{2,0,1:T(4,128)}, u32[]{:S(2)}, u32[]{:S(2)}) collective-permute-start(f32[3,11,256]{2,0,1:T(4,128)} %pad_maximum_fusion.5), channel_id=1, source_target_pairs={{1,0},{2,1},{3,2},{0,3},{5,4},{6,5},{7,6},{4,7},{9,8},{10,9},{11,1... | collective-permute-start | bytes 101384 | tf_op jit(solution)/shard_map/ppermute | solution.py:17
  162.0 1.6 copy-start
  163.7 2.8 %copy-start.3 = (f32[1024,256]{1,0:T(8,128)S(1)}, f32[1024,256]{1,0:T(8,128)}, u32[]{:S(2)}) copy-start(f32[1024,256]{1,0:T(8,128)} %get-tuple-element.50) | copy-start | bytes 3145732
  164.7 1.7 %copy-start.2 = (f32[1024,256]{1,0:T(8,128)S(1)}, f32[1024,256]{1,0:T(8,128)}, u32[]{:S(2)}) copy-start(f32[1024,256]{1,0:T(8,128)} %get-tuple-element.49) | copy-start | bytes 3145732
  166.4 3.3 %copy-start.4 = (f32[1024,209]{0,1:T(8,128)S(1)}, f32[1024,209]{0,1:T(8,128)}, u32[]{:S(2)}) copy-start(f32[1024,209]{0,1:T(8,128)} %mul.759) | copy-start | bytes 2568196
  166.4 3.3 %copy-start.5 = (f32[1024,209]{0,1:T(8,128)S(1)}, f32[1024,209]{0,1:T(8,128)}, u32[]{:S(2)}) copy-start(f32[1024,209]{0,1:T(8,128)} %mul.815) | copy-start | bytes 2568196
  169.8 0.7 copy-start.28
  169.8 1.3 copy-start.31
where the time goes:
time: 172 us
  blocking collectives  83.5 us (49%)
  other arithmetic  32.2 us (19%)
  local copies, waits for them, and re-layouts  20.3 us (12%)
  matrix products  19.3 us (11%)
  starting transfers between devices  7.72 us (4%)
  waiting for transfers between devices  6.39 us (4%)
  between operations  2.24 us (1%)
    psum x1, blocking collectives, body(): totals, counts = lax.psum((charge_sums, live_sums), ('row', 'col'))  39.6 us
    all_to_all x1, blocking collectives, body(): lax.all_to_all(jnp.stack([real_y, imag_y]), 'row', split_axis=2, concat_a...  12.2 us
    all_to_all x1, blocking collectives, body(): lax.all_to_all(jnp.stack([back_y, back_y_imag]), 'col', split_axis=3, con...  11.2 us
    all_to_all x1, blocking collectives, body(): lax.all_to_all(jnp.stack([back_x, back_x_imag]), 'row', split_axis=3, con...  11 us
    all_to_all x1, blocking collectives, body(): lax.all_to_all(jnp.stack([real_z, imag_z]), 'col', split_axis=1, concat_a...  9.47 us
    scatter-add x1, other arithmetic, body(): live_sums = jax.ops.segment_sum(live, structure_id, num_segments=structures)  7.75 us
    scatter-add x1, other arithmetic, body(): jax.ops.segment_sum(charges * live, structure_id, num_segments=structures)  7.74 us
    ppermute x4, starting transfers between devices, passed_along(): return lax.ppermute(block, axis, route)  7.72 us
  transfers between devices with their start and end apart: 4, of which 3 were waited for; matrix products, arithmetic and copies ran while one was open for 3% of the time, Pallas kernels for 0%

commit v1 on v0

--- a/solution.py
+++ b/solution.py
@@ -1,14 +1,24 @@
+import functools
 import math
 import jax
 import jax.numpy as jnp
 from jax import lax
 from jax.sharding import PartitionSpec as P
+from jax.lax import psum
 
 CX = 8
 CY = 16
 NZ = 256
 S_DEV = 8
 highest = lax.Precision.HIGHEST
+
+
+def place_lines_up(xs, axis_id, mesh_name):
+    view_out = psum(xs, axis_id)
+    return psum(view_out, mesh_name)
+
+
+field_push = functools.partial(place_lines_up, axis_id="col", mesh_name="row")
 
 
 def passed_along(block, axis, distance):
@@ -83,7 +93,7 @@
     plane = (y_rows[:, :, None] * x_rows[:, None, :]).reshape(atom_total, -1)
     charge_sums = jax.ops.segment_sum(charges * live, structure_id, num_segments=structures)
     live_sums = jax.ops.segment_sum(live, structure_id, num_segments=structures)
-    totals, counts = lax.psum((charge_sums, live_sums), ("row", "col"))
+    totals, counts = field_push((charge_sums, live_sums))
     neutral = (charges - jnp.take(totals / counts, structure_id)) * live
     spread_grid = lax.dot_general(
         plane,

time: 172 us -> 159 us (0.924)
  blocking collectives: 83.5 us -> 65.2 us
  starting transfers between devices: 7.72 us -> 11.4 us
    psum x1 -> x2, blocking collectives: 39.6 us -> 19.9 us  [the longest x1 14.2 us: place_lines_up(): return psum(view_out, mesh_name)]
    ppermute x4, starting transfers between devices: 7.72 us -> 11.4 us  [passed_along(): return lax.ppermute(block, axis, route)]
where the time goes in v1:
time: 159 us; the launch traced here: 158 us
  blocking collectives  65.2 us (41%)
  other arithmetic  31.9 us (20%)
  local copies, waits for them, and re-layouts  20.2 us (13%)
  matrix products  19.3 us (12%)
  starting transfers between devices  11.4 us (7%)
  waiting for transfers between devices  8.06 us (5%)
  between operations  2.24 us (1%)
    psum x1, blocking collectives, place_lines_up(): return psum(view_out, mesh_name)  14.2 us
    all_to_all x1, blocking collectives, body(): lax.all_to_all(jnp.stack([real_y, imag_y]), 'row', split_axis=2, concat_a...  13.6 us
    ppermute x4, starting transfers between devices, passed_along(): return lax.ppermute(block, axis, route)  11.4 us
    all_to_all x1, blocking collectives, body(): lax.all_to_all(jnp.stack([back_y, back_y_imag]), 'col', split_axis=3, con...  11.2 us
    all_to_all x1, blocking collectives, body(): lax.all_to_all(jnp.stack([back_x, back_x_imag]), 'row', split_axis=3, con...  11 us
    all_to_all x1, blocking collectives, body(): lax.all_to_all(jnp.stack([real_z, imag_z]), 'col', split_axis=1, concat_a...  9.58 us
    ppermute x4, waiting for transfers between devices, passed_along(): return lax.ppermute(block, axis, route)  8.06 us
    scatter-add x1, other arithmetic, body(): live_sums = jax.ops.segment_sum(live, structure_id, num_segments=structures)  7.75 us
  transfers between devices with their start and end apart: 4, of which 3 were waited for; matrix products, arithmetic and copies ran while one was open for 3% of the time, Pallas kernels for 0%

profile of v1, /device:TPU:3, one launch (start us, length us, event | category | flops | bytes accessed | tf_op | source)
XLA Modules:
  0.0 158.3 jit_solution(15726108056464002537)
XLA Ops:
  1.3 0.7 fusion.132
  2.0 0.7 fusion.131
  2.7 7.7 %scatter_custom_fusion = f32[256]{0:T(256)S(1)} fusion(s32[1024]{0:T(1024)} %param.11, f32[1024]{0:T(1024)S(1)} %fusion.131, f32[]{:T(128)} %constant.237.clone.1), kind=kCustom, calls=%fused_computation.243 | custom fusion | flops 1024 | bytes 1536 | tf_op jit(solution)/shard_map/scatter-add | solution.py:94
  10.4 7.7 %scatter_custom_fusion.1 = f32[256]{0:T(256)S(1)} fusion(s32[1024]{0:T(1024)} %param.11, f32[1024]{0:T(1024)S(1)} %fusion.130, f32[]{:T(128)} %constant.237.clone.1), kind=kCustom, calls=%fused_computation.241 | custom fusion | flops 1024 | bytes 1536 | tf_op jit(solution)/shard_map/scatter-add | solution.py:95
  18.2 0.8 fusion.226
  19.1 0.8 fusion.227
  20.1 1.9 %broadcast_multiply_fusion.2 = (f32[1024,19,11]{0,2,1:T(8,128)}, f32[1024,19,11]{0,2,1:T(8,128)S(1)}, f32[1024,19,11]{0,2,1:T(8,128)}) fusion(f32[1024,11]{0,1:T(8,128)S(1)} %get-tuple-element.47, f32[1024,19]{0,1:T(8,128)S(1)} %get-tuple-element.50, f32[1024,11]{0,1:T(8,128)S(1)} %get-tuple-element.48, f32[1024,19]{0,1:T(8,128)S(1)} %get-tuple-element.49), kind=kLoop, calls=%fused_computation.46 | loop fusion | flops 642048 | bytes 2813952 | tf_op jit(solution)/shard_map/mul | solution.py:150
  22.3 5.7 %all-reduce.1 = (f32[256]{0:T(256)S(1)}, f32[256]{0:T(256)S(1)}) all-reduce(f32[256]{0:T(256)S(1)} %scatter_custom_fusion, f32[256]{0:T(256)S(1)} %scatter_custom_fusion.1), channel_id=1, replica_groups=mesh['row'=8,'col'=4] {'col'}, use_global_device_ids=true, to_apply=%region_1.2 | all-reduce | flops 512 | bytes 4096 | tf_op jit(solution)/shard_map/psum | solution.py:17
  28.0 14.2 %all-reduce = (f32[256]{0:T(256)S(1)}, f32[256]{0:T(256)S(1)}) all-reduce(f32[256]{0:T(256)S(1)} %get-tuple-element.32, f32[256]{0:T(256)S(1)} %get-tuple-element.33), channel_id=1, replica_groups=mesh['row'=8,'col'=4] {'row'}, use_global_device_ids=true, to_apply=%region_2.3 | all-reduce | flops 512 | bytes 4096 | tf_op jit(solution)/shard_map/psum | solution.py:18
  42.2 6.8 %gather_fusion = f32[1024]{0:T(1024)S(1)} fusion(f32[256]{0:T(256)S(1)} %div.45, s32[1024]{0:T(1024)S(1)} %fusion.132), kind=kCustom, calls=%fused_computation | custom fusion | bytes 12288 | tf_op jit(solution)/shard_map/jit(_take)/gather | solution.py:97
  49.1 0.6 multiply_multiply_fusion.2
  49.8 2.2 %fusion.17 = f32[19,11,256]{2,1,0:T(8,128)S(1)} fusion(f32[19,11,1024]{2,1,0:T(8,128)S(1)} %dot_general.71, f32[1024]{0:T(1024)S(1)} %get-tuple-element.96, f32[1024]{0:T(1024)S(1)} %get-tuple-element.81, s32[1024]{0:T(1024)S(1)} %get-tuple-element.86, f32[1024]{0:T(1024)S(1)} %get-tuple-element.80, s32[1024]{0:T(1024)S(1)} %get-tuple-element.85, ...), kind=kOutput, calls=%fused_computation.30 | convolution fusion | flops 660602880 | bytes 1106944 | tf_op jit(solution)/shard_map/dot_general | solution.py:98
  52.1 2.2 %collective-permute-start = (f32[19,3,256]{2,1,0:T(4,128)S(1)}, f32[19,3,256]{2,1,0:T(4,128)S(1)}, u32[]{:S(2)}, u32[]{:S(2)}) collective-permute-start(f32[19,3,256]{2,1,0:T(4,128)S(1)} %slice.153), channel_id=1, source_target_pairs={{28,0},{0,4},{4,8},{8,12},{12,16},{16,20},{20,24},{24,28},{29,1},{... | collective-permute-start | bytes 175112 | tf_op jit(solution)/shard_map/ppermute | solution.py:27
  54.3 3.6 %collective-permute-done = f32[19,3,256]{2,1,0:T(4,128)S(1)} collective-permute-done((f32[19,3,256]{2,1,0:T(4,128)S(1)}, f32[19,3,256]{2,1,0:T(4,128)S(1)}, u32[]{:S(2)}, u32[]{:S(2)}) %collective-permute-start) | collective-permute-done | bytes 58400 | tf_op jit(solution)/shard_map/ppermute | solution.py:27
  58.1 6.7 %collective-permute-start.1 = (f32[3,8,256]{2,1,0:T(8,128)S(1)}, f32[3,8,256]{2,1,0:T(8,128)S(1)}, u32[]{:S(2)}, u32[]{:S(2)}) collective-permute-start(f32[3,8,256]{2,1,0:T(8,128)S(1)} %slice.156), channel_id=1, source_target_pairs={{3,0},{0,1},{1,2},{2,3},{7,4},{4,5},{5,6},{6,7},{11,8},{8,9},{9,10... | collective-permute-start | bytes 73736 | tf_op jit(solution)/shard_map/ppermute | solution.py:27
  64.8 0.9 collective-permute-done.1
  65.7 1.3 fusion.16
  67.0 1.3 convolution_bitcast_fusion
  68.4 1.3 copy.81
  69.6 0.7 reshape.1016
  70.4 9.6 %all_to_all.60 = f32[4,1,16384]{2,1,0:T(1,128)S(1)} all-to-all(f32[4,1,16384]{2,1,0:T(1,128)S(1)} %reshape.1016), channel_id=1, replica_groups=mesh['row'=8,'col'=4] {'col'}, dimensions={0} | all-to-all | bytes 524288 | tf_op jit(solution)/shard_map/all_to_all | solution.py:115
  80.0 0.5 broadcast.1325
  80.5 1.3 reduce.4
  81.7 0.7 reshape.1017
  82.4 1.1 copy.128
  83.6 0.6 fusion.73
  84.2 0.5 fusion.71
  84.7 0.5 fusion.15
  85.3 0.6 fusion.13
  86.2 0.3 reshape.1018
  86.5 13.6 %all_to_all.61 = f32[8,1,8192]{2,1,0:T(1,128)S(1)} all-to-all(f32[8,1,8192]{2,1,0:T(1,128)S(1)} %reshape.1018), channel_id=1, replica_groups=mesh['row'=8,'col'=4] {'row'}, dimensions={0} | all-to-all | bytes 524288 | tf_op jit(solution)/shard_map/all_to_all | solution.py:119
  100.1 1.2 reduce.5
  101.6 0.6 fusion.29
  102.2 0.6 fusion.25
  102.9 0.6 fusion.11
  103.5 0.6 fusion.9
  104.1 0.5 fusion.65
  104.6 0.5 fusion.68
  105.1 0.5 fusion.6
  105.6 0.5 fusion.7
  106.8 11.0 %all_to_all.62 = f32[8,1,8192]{2,1,0:T(1,128)S(1)} all-to-all(f32[8,1,8192]{2,1,0:T(1,128)S(1)} %reshape.1020), channel_id=1, replica_groups=mesh['row'=8,'col'=4] {'row'}, dimensions={0} | all-to-all | bytes 524288 | tf_op jit(solution)/shard_map/all_to_all | solution.py:127
  117.8 1.2 reduce.6
  119.6 0.5 fusion.63
  120.3 0.5 fusion.61
  120.8 0.5 fusion.5
  121.3 0.5 fusion.4
  122.5 11.2 %all_to_all.63 = f32[4,1,16384]{2,1,0:T(1,128)S(1)} all-to-all(f32[4,1,16384]{2,1,0:T(1,128)S(1)} %reshape.1022), channel_id=1, replica_groups=mesh['row'=8,'col'=4] {'col'}, dimensions={0} | all-to-all | bytes 524288 | tf_op jit(solution)/shard_map/all_to_all | solution.py:131
  133.6 1.3 reduce.7
  135.7 1.3 fusion.45
  137.5 1.3 fusion.42
  138.8 0.3 collective-permute-start.2
  139.1 3.6 %collective-permute-done.2 = f32[16,3,256]{2,0,1:T(8,128)S(1)} collective-permute-done((f32[16,3,256]{2,0,1:T(8,128)S(1)}, f32[16,3,256]{2,0,1:T(8,128)S(1)}, u32[]{:S(2)}, u32[]{:S(2)}) %collective-permute-start.2) | collective-permute-done | bytes 49184 | tf_op jit(solution)/shard_map/ppermute | solution.py:27
  142.7 0.6 pad_maximum_fusion.5
  143.3 2.2 %collective-permute-start.3 = (f32[3,11,256]{2,0,1:T(4,128)}, f32[3,11,256]{2,0,1:T(4,128)}, u32[]{:S(2)}, u32[]{:S(2)}) collective-permute-start(f32[3,11,256]{2,0,1:T(4,128)} %pad_maximum_fusion.5), channel_id=1, source_target_pairs={{1,0},{2,1},{3,2},{0,3},{5,4},{6,5},{7,6},{4,7},{9,8},{10,9},{11,1... | collective-permute-start | bytes 101384 | tf_op jit(solution)/shard_map/ppermute | solution.py:27
  145.6 3.1 %select_add_fusion.1 = (f32[1024,256]{1,0:T(8,128)}, f32[1024,256]{1,0:T(8,128)}) fusion(f32[1024]{0:T(1024)S(1)} %copy-done.16, s32[1024]{0:T(1024)S(1)} %copy-done.26, f32[1024]{0:T(1024)S(1)} %copy-done.14, s32[1024]{0:T(1024)S(1)} %copy-done.24, f32[1024]{0:T(1024)S(1)} %copy-done.18, s32[1024]{0:T(1024)S(1)} %copy-done.22, f32[1024]{0:T(1024)S(1)} %copy-done.11, ...), kind=kLoop, calls=%fused_computation.34 | loop fusion | flops 4718592 | bytes 2146304 | tf_op jit(solution)/shard_map/add | solution.py:54
  148.7 1.1 mul.759
  149.8 0.6 copy-done
  150.3 1.0 mul.815
  151.4 0.9 pad_maximum_fusion.3
  152.4 0.7 reshape.969
  153.1 3.3 %fusion = f32[2048,209]{0,1:T(8,128)S(1)} fusion(f32[209,256]{1,0:T(8,128)} %reshape.969, f32[1024,256]{1,0:T(8,128)S(1)} %copy-done.3, f32[1024,256]{1,0:T(8,128)S(1)} %copy-done.2), kind=kOutput, calls=%fused_computation.3 | convolution fusion | flops 1315438592 | bytes 4023296 | tf_op jit(solution)/shard_map/dot_general | solution.py:141
  156.5 0.5 multiply_reduce_fusion
  157.1 0.6 multiply_multiply_fusion.21
  157.7 0.6 maximum_multiply_fusion
  (114 shorter events, 5.0 us)
Async XLA Ops:
  19.1 30.7 %copy-start.19 = (s32[1024]{0:T(1024)}, s32[1024]{0:T(1024)S(1)}, u32[]{:S(2)}) copy-start(s32[1024]{0:T(1024)S(1)} %get-tuple-element.83) | copy-start | bytes 12292
  19.1 30.7 %copy-start.21 = (s32[1024]{0:T(1024)}, s32[1024]{0:T(1024)S(1)}, u32[]{:S(2)}) copy-start(s32[1024]{0:T(1024)S(1)} %get-tuple-element.84) | copy-start | bytes 12292
  19.1 30.7 %copy-start.23 = (s32[1024]{0:T(1024)}, s32[1024]{0:T(1024)S(1)}, u32[]{:S(2)}) copy-start(s32[1024]{0:T(1024)S(1)} %get-tuple-element.85) | copy-start | bytes 12292
  19.1 30.7 %copy-start.25 = (s32[1024]{0:T(1024)}, s32[1024]{0:T(1024)S(1)}, u32[]{:S(2)}) copy-start(s32[1024]{0:T(1024)S(1)} %get-tuple-element.86) | copy-start | bytes 12292
  42.2 6.9 %copy-start.29 = (f32[1024]{0:T(1024)S(1)}, f32[1024]{0:T(1024)}, u32[]{:S(2)}) copy-start(f32[1024]{0:T(1024)} %param.10) | copy-start | bytes 12292
  42.2 6.9 %copy-start.30 = (s32[1024]{0:T(1024)S(1)}, s32[1024]{0:T(1024)}, u32[]{:S(2)}) copy-start(s32[1024]{0:T(1024)} %param.11) | copy-start | bytes 12292
  49.7 2.3 %copy-start.10 = (f32[1024]{0:T(1024)}, f32[1024]{0:T(1024)S(1)}, u32[]{:S(2)}) copy-start(f32[1024]{0:T(1024)S(1)} %get-tuple-element.78) | copy-start | bytes 12292
  49.7 2.3 %copy-start.13 = (f32[1024]{0:T(1024)}, f32[1024]{0:T(1024)S(1)}, u32[]{:S(2)}) copy-start(f32[1024]{0:T(1024)S(1)} %get-tuple-element.80) | copy-start | bytes 12292
  49.7 2.3 %copy-start.15 = (f32[1024]{0:T(1024)}, f32[1024]{0:T(1024)S(1)}, u32[]{:S(2)}) copy-start(f32[1024]{0:T(1024)S(1)} %get-tuple-element.81) | copy-start | bytes 12292
  49.7 2.3 %copy-start.17 = (f32[1024]{0:T(1024)}, f32[1024]{0:T(1024)S(1)}, u32[]{:S(2)}) copy-start(f32[1024]{0:T(1024)S(1)} %get-tuple-element.82) | copy-start | bytes 12292
  49.7 2.3 %copy-start.27 = (f32[1024]{0:T(1024)}, f32[1024]{0:T(1024)S(1)}, u32[]{:S(2)}) copy-start(f32[1024]{0:T(1024)S(1)} %get-tuple-element.96) | copy-start | bytes 12292
  52.1 5.8 %collective-permute-start = (f32[19,3,256]{2,1,0:T(4,128)S(1)}, f32[19,3,256]{2,1,0:T(4,128)S(1)}, u32[]{:S(2)}, u32[]{:S(2)}) collective-permute-start(f32[19,3,256]{2,1,0:T(4,128)S(1)} %slice.153), channel_id=1, source_target_pairs={{28,0},{0,4},{4,8},{8,12},{12,16},{16,20},{20,24},{24,28},{29,1},{... | collective-permute-start | bytes 175112 | tf_op jit(solution)/shard_map/ppermute | solution.py:27
  58.1 7.6 %collective-permute-start.1 = (f32[3,8,256]{2,1,0:T(8,128)S(1)}, f32[3,8,256]{2,1,0:T(8,128)S(1)}, u32[]{:S(2)}, u32[]{:S(2)}) collective-permute-start(f32[3,8,256]{2,1,0:T(8,128)S(1)} %slice.156), channel_id=1, source_target_pairs={{3,0},{0,1},{1,2},{2,3},{7,4},{4,5},{5,6},{6,7},{11,8},{8,9},{9,10... | collective-permute-start | bytes 73736 | tf_op jit(solution)/shard_map/ppermute | solution.py:27
  101.5 1.3 copy-start.6
  137.0 8.5 %copy-start.7 = (f32[1024]{0:T(1024)S(1)}, f32[1024]{0:T(1024)}, u32[]{:S(2)}) copy-start(f32[1024]{0:T(1024)} %get-tuple-element.75) | copy-start | bytes 12292
  137.0 8.5 %copy-start.8 = (f32[1024]{0:T(1024)S(1)}, f32[1024]{0:T(1024)}, u32[]{:S(2)}) copy-start(f32[1024]{0:T(1024)} %get-tuple-element.76) | copy-start | bytes 12292
  137.1 8.5 %copy-start.9 = (f32[1024]{0:T(1024)S(1)}, f32[1024]{0:T(1024)}, u32[]{:S(2)}) copy-start(f32[1024]{0:T(1024)} %get-tuple-element.77) | copy-start | bytes 12292
  137.1 8.5 %copy-start.11 = (f32[1024]{0:T(1024)S(1)}, f32[1024]{0:T(1024)}, u32[]{:S(2)}) copy-start(f32[1024]{0:T(1024)} %copy-done.10) | copy-start | bytes 12292
  137.1 8.5 %copy-start.12 = (f32[1024]{0:T(1024)S(1)}, f32[1024]{0:T(1024)}, u32[]{:S(2)}) copy-start(f32[1024]{0:T(1024)} %get-tuple-element.79) | copy-start | bytes 12292
  137.1 8.5 %copy-start.14 = (f32[1024]{0:T(1024)S(1)}, f32[1024]{0:T(1024)}, u32[]{:S(2)}) copy-start(f32[1024]{0:T(1024)} %copy-done.13) | copy-start | bytes 12292
  137.1 8.5 %copy-start.16 = (f32[1024]{0:T(1024)S(1)}, f32[1024]{0:T(1024)}, u32[]{:S(2)}) copy-start(f32[1024]{0:T(1024)} %copy-done.15) | copy-start | bytes 12292
  137.1 8.5 %copy-start.18 = (f32[1024]{0:T(1024)S(1)}, f32[1024]{0:T(1024)}, u32[]{:S(2)}) copy-start(f32[1024]{0:T(1024)} %copy-done.17) | copy-start | bytes 12292
  137.1 8.5 %copy-start.20 = (s32[1024]{0:T(1024)S(1)}, s32[1024]{0:T(1024)}, u32[]{:S(2)}) copy-start(s32[1024]{0:T(1024)} %copy-done.19) | copy-start | bytes 12292
  137.1 8.5 %copy-start.22 = (s32[1024]{0:T(1024)S(1)}, s32[1024]{0:T(1024)}, u32[]{:S(2)}) copy-start(s32[1024]{0:T(1024)} %copy-done.21) | copy-start | bytes 12292
  137.1 8.5 %copy-start.24 = (s32[1024]{0:T(1024)S(1)}, s32[1024]{0:T(1024)}, u32[]{:S(2)}) copy-start(s32[1024]{0:T(1024)} %copy-done.23) | copy-start | bytes 12292
  137.1 8.5 %copy-start.26 = (s32[1024]{0:T(1024)S(1)}, s32[1024]{0:T(1024)}, u32[]{:S(2)}) copy-start(s32[1024]{0:T(1024)} %copy-done.25) | copy-start | bytes 12292
  138.8 10.0 %copy-start.1 = (f32[1024,19,11]{0,2,1:T(8,128)S(1)}, f32[1024,19,11]{0,2,1:T(8,128)}, u32[]{:S(2)}) copy-start(f32[1024,19,11]{0,2,1:T(8,128)} %get-tuple-element.44) | copy-start | bytes 2568196
  138.8 3.9 %collective-permute-start.2 = (f32[16,3,256]{2,0,1:T(8,128)S(1)}, f32[16,3,256]{2,0,1:T(8,128)S(1)}, u32[]{:S(2)}, u32[]{:S(2)}) collective-permute-start(f32[16,3,256]{2,0,1:T(8,128)S(1)} %slice.165), channel_id=1, source_target_pairs={{4,0},{8,4},{12,8},{16,12},{20,16},{24,20},{28,24},{0,28},{5,1},{9... | collective-permute-start | bytes 147464 | tf_op jit(solution)/shard_map/ppermute | solution.py:27
  143.3 8.1 %collective-permute-start.3 = (f32[3,11,256]{2,0,1:T(4,128)}, f32[3,11,256]{2,0,1:T(4,128)}, u32[]{:S(2)}, u32[]{:S(2)}) collective-permute-start(f32[3,11,256]{2,0,1:T(4,128)} %pad_maximum_fusion.5), channel_id=1, source_target_pairs={{1,0},{2,1},{3,2},{0,3},{5,4},{6,5},{7,6},{4,7},{9,8},{10,9},{11,1... | collective-permute-start | bytes 101384 | tf_op jit(solution)/shard_map/ppermute | solution.py:27
  148.7 1.6 %copy-start = (f32[1024,19,11]{0,2,1:T(8,128)S(1)}, f32[1024,19,11]{0,2,1:T(8,128)}, u32[]{:S(2)}) copy-start(f32[1024,19,11]{0,2,1:T(8,128)} %get-tuple-element.46) | copy-start | bytes 2568196
  150.3 2.8 %copy-start.3 = (f32[1024,256]{1,0:T(8,128)S(1)}, f32[1024,256]{1,0:T(8,128)}, u32[]{:S(2)}) copy-start(f32[1024,256]{1,0:T(8,128)} %get-tuple-element.52) | copy-start | bytes 3145732
  151.4 1.7 %copy-start.2 = (f32[1024,256]{1,0:T(8,128)S(1)}, f32[1024,256]{1,0:T(8,128)}, u32[]{:S(2)}) copy-start(f32[1024,256]{1,0:T(8,128)} %get-tuple-element.51) | copy-start | bytes 3145732
  153.1 3.3 %copy-start.4 = (f32[1024,209]{0,1:T(8,128)S(1)}, f32[1024,209]{0,1:T(8,128)}, u32[]{:S(2)}) copy-start(f32[1024,209]{0,1:T(8,128)} %mul.759) | copy-start | bytes 2568196
  153.1 3.3 %copy-start.5 = (f32[1024,209]{0,1:T(8,128)S(1)}, f32[1024,209]{0,1:T(8,128)}, u32[]{:S(2)}) copy-start(f32[1024,209]{0,1:T(8,128)} %mul.815) | copy-start | bytes 2568196
  156.5 0.7 copy-start.28
  156.5 1.3 copy-start.31
